TPU v7x, 32 devices: a whole 2x2x4 slice. The times are simulated.
32 devices in a mesh: frames: 16 (over z, y, core), dp: 2 (over x).
Axes of the slice: x: 2, y: 2, z: 4, core: 2. Of those that a mesh axis runs over, the one named last changes fastest.
Arguments:
- shifted: bfloat16 [2, 64, 16, 16, 640], P('dp', 'frames'), may hold values from -6 to 6
- out_grad: bfloat16 [2, 64, 16, 16, 640], P('dp', 'frames'), may hold values from -6 to 6
- conv_weight: bfloat16 [640, 5760], P('frames'), may hold values from -0.078125 to 0.078125
- norm_gain: float32 [640], replicated, may hold values from 0.5 to 2
- norm_bias: float32 [640], replicated, may hold values from -4 to 4
- shift_fwd: int32 [80], replicated, may hold values from 0 to 639, as said below
- shift_bwd: int32 [80], replicated, may hold values from 0 to 639, as said below
Outputs:
- in_grad: bfloat16 [2, 64, 16, 16, 640], P('dp', 'frames')
- weight_grad: float32 [640, 5760], P('frames')
- gain_grad: float32 [640], replicated
- bias_grad: float32 [640], replicated
Inputs may be any that keep to these rules, and one draw needn't show every extreme that they name: `shift_fwd`: 80 distinct channel numbers, none of them in shift_bwd. `shift_bwd`: 80 distinct channel numbers, none of them in shift_fwd.
All inputs are finite; a program needn't handle non-finite values.
Results may differ from a plain program's by a relative error of at most 0.003.
Values may be sent and summed in bfloat16 or wider, within the bound.
No kernel may reach another device: no remote copies, remote signals or barrier semaphores. Data moves between devices by JAX's collectives and lax.ppermute only.
A program may use at most 128 MiB of HBM per device.

v0:
```python
import jax
import jax.numpy as jnp
from jax import lax
from jax.sharding import PartitionSpec as P

GROUP_CH = 20
epsilon = 1e-05


def with_halo(x, sides, width):
    for axis, dim in sides:
        size, length = (lax.axis_size(axis), x.shape[dim])
        up = [(i, (i + 1) % size) for i in range(size - 1)]
        down = [(j, i) for i, j in up]
        last = lax.slice_in_dim(x, length - width, length, axis=dim)
        first = lax.slice_in_dim(x, 0, width, axis=dim)
        before = lax.ppermute(last, axis, up)
        after = lax.ppermute(first, axis, down)
        x = jnp.concatenate([before, x, after], axis=dim)
    return x


def pad_space(values):
    return jnp.pad(values, ((0, 0), (1, 1), (1, 1), (0, 0)))


def on_device(shifted, out_grad, conv_weight, norm_gain, norm_bias, shift_fwd, shift_bwd):
    frames_local = shifted[0]
    grad_local = out_grad[0]
    frame_count, row_count, col_count, channels = frames_local.shape
    groups = channels // GROUP_CH
    whole_weight = lax.all_gather(conv_weight, "frames", axis=0, tiled=True)
    values = frames_local.astype(jnp.float32).reshape(
        frame_count, row_count * col_count, groups, GROUP_CH
    )
    center = jnp.mean(values, axis=(1, 3), keepdims=True)
    spread = jnp.mean(jnp.square(values - center), axis=(1, 3), keepdims=True)
    inverse = lax.rsqrt(spread + epsilon)
    grouped_normed = (values - center) * inverse
    normed = grouped_normed.reshape(frame_count, row_count, col_count, channels)
    before = normed * norm_gain + norm_bias
    activation = jax.nn.silu(before).astype(jnp.bfloat16)
    act_padded = pad_space(activation)
    grad_padded = pad_space(grad_local)
    grad_rows = grad_local.reshape(-1, channels)
    act_grad = jnp.zeros((grad_rows.shape[0], channels), jnp.float32)
    for tap_index in range(9):
        row_off, col_off = divmod(tap_index, 3)
        grad_view = grad_padded[
            :, 2 - row_off : 2 - row_off + row_count, 2 - col_off : 2 - col_off + col_count, :
        ].reshape(-1, channels)
        act_grad = act_grad + jnp.dot(
            grad_view,
            whole_weight[:, tap_index * channels : (tap_index + 1) * channels],
            preferred_element_type=jnp.float32,
        )
    scale = float(
        lax.axis_size("dp") * lax.axis_size("frames") * frame_count * row_count * col_count
    ) ** (-0.5)
    parts = []
    for tap_index in range(9):
        row_off, col_off = divmod(tap_index, 3)
        act_view = act_padded[
            :, row_off : row_off + row_count, col_off : col_off + col_count, :
        ].reshape(-1, channels)
        parts.append(
            lax.dot_general(
                grad_rows, act_view, (((0,), (0,)), ((), ())), preferred_element_type=jnp.float32
            )
        )
    kernel_piece = lax.psum_scatter(
        jnp.concatenate(parts, axis=1), ("frames", "dp"), scatter_dimension=0, tiled=True
    )
    kernel_shard = lax.all_gather(kernel_piece, "dp", axis=0, tiled=True)
    weight_grad = kernel_shard * scale
    sigmoid_val = jax.nn.sigmoid(before)
    pre_grad = act_grad.reshape(before.shape) * sigmoid_val * (1.0 + before * (1.0 - sigmoid_val))
    gain_part = jnp.sum(pre_grad * normed, axis=(0, 1, 2))
    bias_part = jnp.sum(pre_grad, axis=(0, 1, 2))
    gain_total, bias_total = lax.psum((gain_part, bias_part), ("frames", "dp"))
    norm_grad = (pre_grad * norm_gain).reshape(values.shape)
    first_mean = jnp.mean(norm_grad, axis=(1, 3), keepdims=True)
    second_mean = jnp.mean(norm_grad * grouped_normed, axis=(1, 3), keepdims=True)
    shifted_grad = (
        ((norm_grad - first_mean - grouped_normed * second_mean) * inverse)
        .reshape(frames_local.shape)
        .astype(jnp.bfloat16)
    )
    channel_ids = jnp.arange(channels, dtype=jnp.int32)
    forward_match = channel_ids[None, :] == shift_fwd[:, None]
    backward_match = channel_ids[None, :] == shift_bwd[:, None]
    forward_select = forward_match.astype(jnp.bfloat16)
    backward_select = backward_match.astype(jnp.bfloat16)
    forward_mask = jnp.any(forward_match, axis=0)
    backward_mask = jnp.any(backward_match, axis=0)
    plane = row_count * col_count
    first_frame = shifted_grad[0].reshape(plane, channels)
    last_frame = shifted_grad[frame_count - 1].reshape(plane, channels)
    contract_channels = (((1,), (1,)), ((), ()))
    rim_first = lax.dot_general(
        forward_select, first_frame, contract_channels, preferred_element_type=jnp.float32
    ).astype(jnp.bfloat16)
    rim_last = lax.dot_general(
        backward_select, last_frame, contract_channels, preferred_element_type=jnp.float32
    ).astype(jnp.bfloat16)
    extended = with_halo(jnp.stack([rim_first, rim_last]), (("frames", 0),), 1)
    contract_fold = (((0,), (0,)), ((), ()))
    from_prev = lax.dot_general(
        extended[0], backward_select, contract_fold, preferred_element_type=jnp.float32
    ).astype(jnp.bfloat16)
    from_next = lax.dot_general(
        extended[3], forward_select, contract_fold, preferred_element_type=jnp.float32
    ).astype(jnp.bfloat16)
    from_prev = from_prev.reshape(1, row_count, col_count, channels)
    from_next = from_next.reshape(1, row_count, col_count, channels)
    later = jnp.concatenate([shifted_grad[1:], from_next], axis=0)
    earlier = jnp.concatenate([from_prev, shifted_grad[:-1]], axis=0)
    in_grad = jnp.where(forward_mask, later, jnp.where(backward_mask, earlier, shifted_grad))
    return (in_grad[None], weight_grad, gain_total * scale, bias_total * scale)


def solution(mesh):
    in_specs = (
        P("dp", "frames", None, None, None),
        P("dp", "frames", None, None, None),
        P("frames", None),
        P(),
        P(),
        P(),
        P(),
    )
    out_specs = (P("dp", "frames", None, None, None), P("frames", None), P(), P())
    return jax.shard_map(
        on_device, mesh=mesh, in_specs=in_specs, out_specs=out_specs, check_vma=False
    )
```

profile of v0, /device:TPU:0, one launch (start us, length us, event | category | flops | bytes accessed | tf_op | source)
XLA Modules:
  0.0 428.5 jit_solution(4472811872331687543)
XLA Ops:
  7.2 0.7 all-gather.3.cloned.1.call-update
  8.0 21.9 %reshape.226 = f32[4,256,32,20]{3,2,1,0:T(8,128)} reshape(bf16[1,4,16,16,640]{4,3,2,1,0:T(8,128)(2,1)} %param.7) | data formatting | bytes 3932160 | tf_op jit(solution)/shard_map/convert_element_type | solution.py:33
  29.9 0.2 convert_reduce_fusion
  30.1 0.1 reduce_sum.69
  30.2 0.1 reduce_sum.70
  30.3 0.1 copy.31
  30.5 0.1 sub.85
  30.6 0.4 multiply_reduce_fusion.2
  31.0 0.1 reduce_sum.72
  31.1 0.1 reduce_sum.73
  31.2 0.1 copy.33
  31.3 0.1 mul.189
  31.4 0.1 mul.190
  31.5 11.4 %copy.32 = f32[4,256,32,20]{1,0,3,2:T(4,128)} copy(f32[4,256,32,20]{3,2,1,0:T(8,128)} %reshape.226) | data formatting | bytes 5242880 | tf_op jit(solution)/shard_map/convert_element_type | solution.py:33
  42.9 0.1 add.132
  43.0 0.1 mul.201
  43.1 8.4 %pad_slice_fusion.8 = (bf16[4,16,16,640]{3,2,1,0:T(8,128)(2,1)S(1)}, bf16[4,16,16,640]{3,2,1,0:T(8,128)(2,1)}, bf16[4,16,16,640]{3,2,1,0:T(8,128)(2,1)}, bf16[4,...) fusion(bf16[4,16,16,640]{3,2,1,0:T(8,128)(2,1)} %bitcast.130), kind=kLoop, calls=%fused_computation.8 | loop fusion | bytes 11796480 | tf_op jit(solution)/shard_map/slice | solution.py:49
  51.5 29.3 %all-gather.3.cloned.1.call-done = bf16[640,5760]{1,0:T(8,128)(2,1)} async-done(((bf16[40,5760]{1,0:T(8,128)(2,1)}), bf16[640,5760]{1,0:T(8,128)(2,1)}) %all-gather.3.cloned.1.call-update) | async-done | bytes 7372816 | tf_op jit(solution)/shard_map/all_gather | solution.py:32
  80.8 3.0 fusion.4
  83.8 1.1 copy-done.10
  84.9 1.3 fusion.6
  86.3 1.3 fusion.8
  87.6 1.3 fusion.10
  89.0 1.3 fusion.12
  90.3 1.3 fusion.14
  91.7 1.3 fusion.18
  93.0 1.3 fusion.16
  94.3 5.4 %fusion.28 = (f32[640]{0:T(1024)S(1)}, f32[640]{0:T(1024)S(1)}, f32[1024,640]{1,0:T(8,128)}) fusion(f32[4,640]{1,0:T(4,128)S(1)} %mul.190, f32[4,640]{1,0:T(4,128)S(1)} %sub.85, bf16[1,4,16,16,640]{4,3,2,1,0:T(8,128)(2,1)S(1)} %copy-done, f32[640]{0:T(1024)S(1)} %copy-done.11, f32[640]{0:T(1024)S(1)} %copy-done.12, bf16[1024,640]{1,0:T(8,128)(2,1)S(1)} %bitcast.124, ...), kind=kOutput, calls=%fused_computation.87 | convolution fusion | flops 854588160 | bytes 27064320 | tf_op jit(solution)/shard_map/dot_general | solution.py:52
  99.7 3.2 copy.30
  103.0 4.2 reshape.215
  107.1 5.7 %fusion.29 = (f32[4,32]{0,1:T(8,128)S(1)}, f32[4,32]{0,1:T(8,128)S(1)}) fusion(f32[4,32]{0,1:T(8,128)S(1)} %copy.33, f32[4,256,32,20]{1,0,3,2:T(4,128)} %copy.32, f32[4,32]{0,1:T(8,128)S(1)} %copy.31, f32[4,256,32,20]{1,0,3,2:T(4,128)} %reshape.215, f32[32,20]{1,0:T(8,128)S(1)} %add.132, f32[32,20]{1,0:T(8,128)S(1)} %mul.201), kind=kLoop, calls=%fused_computation.88 | loop fusion | flops 10485504 | bytes 5250048 | tf_op jit(solution)/shard_map/reduce_sum | solution.py:82
  112.8 0.1 copy.35
  113.0 0.1 mul.210
  113.3 0.1 sub.95
  113.4 3.6 multiply_convert_fusion
  117.0 3.0 pad_slice_fusion
  120.0 2.4 bitcast_dynamic-update-slice_fusion.8
  122.4 2.4 bitcast_dynamic-update-slice_fusion.7
  124.8 2.4 bitcast_dynamic-update-slice_fusion.6
  127.3 2.4 bitcast_dynamic-update-slice_fusion.5
  129.7 2.4 bitcast_dynamic-update-slice_fusion.4
  132.1 2.4 bitcast_dynamic-update-slice_fusion.3
  134.5 2.5 bitcast_dynamic-update-slice_fusion.2
  137.0 2.4 bitcast_dynamic-update-slice_fusion.1
  139.4 2.4 bitcast_dynamic-update-slice_fusion
  141.9 0.6 copy-done.13
  142.5 0.1 fusion.20
  142.7 0.2 fusion.1
  143.0 1.3 collective-permute-start
  144.3 0.2 fusion.2
  144.5 3.0 collective-permute-start.1
  147.6 42.4 %all-reduce.3 = (f32[640]{0:T(1024)S(1)}, f32[640]{0:T(1024)S(1)}) all-reduce(f32[640]{0:T(1024)S(1)} %get-tuple-element.5, f32[640]{0:T(1024)S(1)} %get-tuple-element.4), channel_id=1, replica_groups=mesh['frames'=16,'dp'=2] {'frames','dp'}, use_global_device_ids=true, to_apply=%region_10.11 | all-reduce | flops 1280 | bytes 10240 | tf_op jit(solution)/shard_map/psum | solution.py:80
  189.9 0.2 slice_bitcast_fusion
  190.1 0.6 broadcast_multiply_fusion.1
  190.7 0.3 convolution_convert_fusion.1
  191.0 0.3 convolution_convert_fusion
  191.3 0.4 copy-done.1
  191.8 3.0 maximum_select_fusion
  194.7 203.1 %all-reduce.6.cloned.1.call-done = f32[640,5760]{0,1:T(8,128)} async-done(((f32[640,5760]{0,1:T(8,128)}), f32[640,5760]{0,1:T(8,128)}) %all-reduce.6.cloned.1.call-update) | async-done | bytes 14745616
  397.9 5.1 %dynamic-slice_bitcast_fusion = f32[1,20,5760]{1,2,0:T(8,128)} fusion(f32[640,5760]{0,1:T(8,128)} %all-reduce.6.cloned.1.call-done, u32[]{:T(128)S(6)} %multiply.25), kind=kLoop, calls=%fused_computation.16 | loop fusion | bytes 921604
  402.9 2.6 copy.36
  405.5 15.0 %all-gather = f32[2,20,5760]{2,1,0:T(8,128)S(1)} all-gather(f32[1,20,5760]{2,1,0:T(8,128)S(1)} %copy.36), channel_id=1, replica_groups=mesh['frames'=16,'dp'=2] {'dp'}, dimensions={0}, use_global_device_ids=true | all-gather | bytes 1382400 | tf_op jit(solution)/shard_map/all_gather | solution.py:74
  420.5 0.1 broadcast_multiply_fusion
  420.6 1.0 reshape.231
  (41 shorter events, 0.6 us)
Async XLA Ops:
  7.2 73.6 %all-gather.3.cloned.1.call-start = ((), (), s32[]{:S(2)}) async-start(), calls=%async_computation | async-start | bytes 7833600 | tf_op jit(solution)/shard_map/all_gather | solution.py:32
  7.9 22.0 %copy-start = (bf16[1,4,16,16,640]{4,3,2,1,0:T(8,128)(2,1)S(1)}, bf16[1,4,16,16,640]{4,3,2,1,0:T(8,128)(2,1)}, u32[]{:S(2)}) copy-start(bf16[1,4,16,16,640]{4,3,2,1,0:T(8,128)(2,1)} %param.7) | copy-start | bytes 3932164
  7.9 389.9 %all-reduce.6.cloned.1.call-start = ((), (), s32[]{:S(2)}) async-start(), calls=%async_computation.1 | async-start | bytes 29491200
  31.5 11.4 %copy-start.11 = (f32[640]{0:T(1024)S(1)}, f32[640]{0:T(1024)}, u32[]{:S(2)}) copy-start(f32[640]{0:T(1024)} %param.11) | copy-start | bytes 7684
  31.5 11.5 %copy-start.12 = (f32[640]{0:T(1024)S(1)}, f32[640]{0:T(1024)}, u32[]{:S(2)}) copy-start(f32[640]{0:T(1024)} %param.10) | copy-start | bytes 7684
  80.8 3.0 copy-start.9
  80.8 4.1 copy-start.10
  84.9 1.3 copy-start.8
  86.2 1.3 copy-start.2
  87.6 1.3 copy-start.7
  88.9 1.3 copy-start.6
  90.3 1.3 copy-start.5
  91.6 1.3 copy-start.4
  117.0 3.0 copy-start.3
  141.9 0.7 copy-start.13
  141.9 0.7 copy-start.14
  143.0 47.7 %collective-permute-start = (bf16[1,80,256]{2,1,0:T(8,128)(2,1)S(1)}, bf16[1,80,256]{2,1,0:T(8,128)(2,1)S(1)}, u32[]{:S(2)}, u32[]{:S(2)}) collective-permute-start(bf16[1,80,256]{2,1,0:T(8,128)(2,1)S(1)} %fusion.1), channel_id=1, source_target_pairs={{2,0},{4,2},{6,4},{8,6},{10,8},{12,10},{14,12},{16,14},{18,16},{20... | collective-permute-start | bytes 122888 | tf_op jit(solution)/shard_map/ppermute | solution.py:18
  144.5 46.5 %collective-permute-start.1 = (bf16[1,80,256]{2,1,0:T(8,128)(2,1)S(1)}, bf16[1,80,256]{2,1,0:T(8,128)(2,1)S(1)}, u32[]{:S(2)}, u32[]{:S(2)}) collective-permute-start(bf16[1,80,256]{2,1,0:T(8,128)(2,1)S(1)} %fusion.2), channel_id=1, source_target_pairs={{0,2},{2,4},{4,6},{6,8},{8,10},{10,12},{12,14},{14,16},{16,18},{18... | collective-permute-start | bytes 122888 | tf_op jit(solution)/shard_map/ppermute | solution.py:17
  189.9 1.8 copy-start.1
Sparse Core Ops, SparseCore 0:
  10.1 70.5 all-gather.2
  142.0 255.7 all-reduce.5
where the time goes:
time: 429 us; the launch traced here: 428 us
  waiting for transfers between devices  233 us (54%)
  local copies, waits for them, and re-layouts  64.8 us (15%)
  blocking collectives  57.4 us (13%)
  matrix products  40.6 us (9%)
  between operations  14.4 us (3%)
  other arithmetic  13.8 us (3%)
  starting transfers between devices  4.4 us (1%)
    unnamed x3, waiting for transfers between devices  204 us
    psum x1, blocking collectives, on_device(): gain_total, bias_total = lax.psum((gain_part, bias_part), ('frames', 'dp'))  42.4 us
    convert_element_type x2, local copies, waits for them, and re-layouts, on_device(): frames_local.astype(jnp.float32)  33.3 us
    all_gather x1, waiting for transfers between devices, on_device(): whole_weight = lax.all_gather(conv_weight, 'frames', axis=0, tiled=True)  29.3 us
    dot_general x9, matrix products, on_device(): lax.dot_general(grad_rows, act_view, (((0,), (0,)), ((), ())), preferred_...  21.8 us
    dot_general x9, matrix products, on_device(): jnp.dot(grad_view, whole_weight[:, tap_index * channels:(tap_index + 1) *...  17.7 us
    all_gather x1, blocking collectives, on_device(): kernel_shard = lax.all_gather(kernel_piece, 'dp', axis=0, tiled=True)  15 us
    unnamed x32, local copies, waits for them, and re-layouts  9.92 us
  transfers between devices with their start and end apart: 4, of which 2 were waited for; matrix products, arithmetic and copies ran while one was open for 11% of the time, Pallas kernels for 0%

commit v1 on v0

--- a/solution.py
+++ b/solution.py
@@ -29,7 +29,24 @@
     grad_local = out_grad[0]
     frame_count, row_count, col_count, channels = frames_local.shape
     groups = channels // GROUP_CH
-    whole_weight = lax.all_gather(conv_weight, "frames", axis=0, tiled=True)
+    ways, here, step = (lax.axis_size("frames"), lax.axis_index("frames"), conv_weight.shape[0])
+    shape = [n * ways if d == 0 else n for d, n in enumerate(conv_weight.shape)]
+    whole_weight = lax.dynamic_update_slice_in_dim(
+        jnp.zeros(shape, conv_weight.dtype), conv_weight, here * step, axis=0
+    )
+    going_up = going_down = conv_weight
+    for far in range(1, ways // 2 + 1):
+        going_up = lax.ppermute(going_up, "frames", [(d, (d + 1) % ways) for d in range(ways)])
+        whole_weight = lax.dynamic_update_slice_in_dim(
+            whole_weight, going_up, (here - far) % ways * step, axis=0
+        )
+        if 2 * far < ways:
+            going_down = lax.ppermute(
+                going_down, "frames", [(d, (d - 1) % ways) for d in range(ways)]
+            )
+            whole_weight = lax.dynamic_update_slice_in_dim(
+                whole_weight, going_down, (here + far) % ways * step, axis=0
+            )
     values = frames_local.astype(jnp.float32).reshape(
         frame_count, row_count * col_count, groups, GROUP_CH
     )

time: 429 us -> 507 us (1.18); the launches traced: 428 us -> 500 us
  starting transfers between devices: 4.4 us -> 48.1 us
  local copies, waits for them, and re-layouts: 64.8 us -> 77.8 us
  matrix products: 40.6 us -> 48.5 us
    ppermute x0 -> x15, starting transfers between devices: none -> 41.8 us  [the longest x8 21.9 us: on_device(): lax.ppermute(going_up, 'frames', [(d, (d + 1) % ways) for d in range(ways)])]
    ppermute x0 -> x15, waiting for transfers between devices: none -> 30.4 us  [the longest x8 30.3 us: on_device(): lax.ppermute(going_up, 'frames', [(d, (d + 1) % ways) for d in range(ways)])]
    all_gather x1 -> x0, waiting for transfers between devices: 29.3 us -> none  [on_device(): whole_weight = lax.all_gather(conv_weight, 'frames', axis=0, tiled=True)]
    dynamic_update_slice x0 -> x16, local copies, waits for them, and re-layouts: none -> 14 us  [the longest x8 7.47 us: on_device(): lax.dynamic_update_slice_in_dim(whole_weight, going_up, (here - far) % wa...]
    dot_general x9, matrix products: 17.7 us -> 25.6 us  [on_device(): jnp.dot(grad_view, whole_weight[:, tap_index * channels:(tap_index + 1) *...]
    slice x1, local copies, waits for them, and re-layouts: 8.36 us -> 3.14 us  [on_device(): grad_padded[:, 2 - row_off:2 - row_off + row_count, 2 - col_off:2 - col_o...]
    unnamed x3 -> x2, waiting for transfers between devices: 204 us -> 204 us
  transfers between devices with their start and end apart: 4 -> 18, of which waited for: 2 -> 8; matrix products, arithmetic and copies ran while one was open for 11% -> 13% of each run, Pallas kernels for 0% -> 0%
where the time goes in v1:
time: 507 us; the launch traced here: 500 us
  waiting for transfers between devices  235 us (46%)
  local copies, waits for them, and re-layouts  77.8 us (15%)
  blocking collectives  59.7 us (12%)
  matrix products  48.5 us (10%)
  starting transfers between devices  48.1 us (9%)
  other arithmetic  16.4 us (3%)
  between operations  14.6 us (3%)
    unnamed x2, waiting for transfers between devices  204 us
    psum x1, blocking collectives, on_device(): gain_total, bias_total = lax.psum((gain_part, bias_part), ('frames', 'dp'))  44.7 us
    convert_element_type x2, local copies, waits for them, and re-layouts, on_device(): frames_local.astype(jnp.float32)  32 us
    ppermute x8, waiting for transfers between devices, on_device(): lax.ppermute(going_up, 'frames', [(d, (d + 1) % ways) for d in range(ways)])  30.3 us
    dot_general x9, matrix products, on_device(): jnp.dot(grad_view, whole_weight[:, tap_index * channels:(tap_index + 1) *...  25.6 us
    ppermute x8, starting transfers between devices, on_device(): lax.ppermute(going_up, 'frames', [(d, (d + 1) % ways) for d in range(ways)])  21.9 us
    dot_general x9, matrix products, on_device(): lax.dot_general(grad_rows, act_view, (((0,), (0,)), ((), ())), preferred_...  21.8 us
    ppermute x7, starting transfers between devices, on_device(): lax.ppermute(going_down, 'frames', [(d, (d - 1) % ways) for d in range(wa...  20 us
  transfers between devices with their start and end apart: 18, of which 8 were waited for; matrix products, arithmetic and copies ran while one was open for 13% of the time, Pallas kernels for 0%

profile of v1, /device:TPU:0, one launch (start us, length us, event | category | flops | bytes accessed | tf_op | source)
XLA Modules:
  0.0 500.0 jit_solution(9053143046980167805)
XLA Ops:
  7.8 5.0 %collective-permute-start.1 = (bf16[40,5760]{1,0:T(8,128)(2,1)}, bf16[40,5760]{1,0:T(8,128)(2,1)S(1)}, u32[]{:S(2)}, u32[]{:S(2)}) collective-permute-start(bf16[40,5760]{1,0:T(8,128)(2,1)} %param.9), channel_id=1, source_target_pairs={{0,30},{2,0},{4,2},{6,4},{8,6},{10,8},{12,10},{14,12},{16,14},{18,... | collective-permute-start | bytes 1382408 | tf_op jit(solution)/shard_map/ppermute | solution.py:44
  12.8 1.5 convert_reduce_fusion
  14.8 1.7 multiply_reduce_fusion.2
  16.7 3.4 broadcast_in_dim.9
  20.9 20.5 %reshape.226 = f32[4,256,32,20]{3,2,1,0:T(8,128)} reshape(bf16[1,4,16,16,640]{4,3,2,1,0:T(8,128)(2,1)S(1)} %copy-done) | data formatting | bytes 3932160 | tf_op jit(solution)/shard_map/convert_element_type | solution.py:50
  43.7 11.5 %copy.37 = f32[4,256,32,20]{1,0,3,2:T(4,128)} copy(f32[4,256,32,20]{3,2,1,0:T(8,128)} %reshape.226) | data formatting | bytes 5242880 | tf_op jit(solution)/shard_map/convert_element_type | solution.py:50
  56.5 3.1 pad_slice_fusion.8
  59.8 4.4 collective-permute-start.3
  64.2 1.8 constant_dynamic-update-slice_fusion.14
  66.8 3.9 collective-permute-done.2
  70.7 4.4 collective-permute-start.5
  75.1 0.8 constant_dynamic-update-slice_fusion.12
  76.0 0.8 constant_dynamic-update-slice_fusion.11
  76.8 4.6 collective-permute-done.4
  82.2 3.6 collective-permute-start.7
  85.9 0.8 constant_dynamic-update-slice_fusion.10
  86.7 0.8 constant_dynamic-update-slice_fusion.9
  87.5 4.6 collective-permute-done.6
  92.1 2.2 collective-permute-start.8
  94.3 2.3 collective-permute-start.9
  97.4 0.8 constant_dynamic-update-slice_fusion.7
  98.2 4.7 collective-permute-done.8
  102.9 4.3 collective-permute-start.10
  107.3 0.8 constant_dynamic-update-slice_fusion.6
  108.9 4.6 collective-permute-done.10
  113.6 6.5 %collective-permute-start.12 = (bf16[40,5760]{1,0:T(8,128)(2,1)S(1)}, bf16[40,5760]{1,0:T(8,128)(2,1)S(1)}, u32[]{:S(2)}, u32[]{:S(2)}) collective-permute-start(bf16[40,5760]{1,0:T(8,128)(2,1)S(1)} %collective-permute-done.10), channel_id=1, source_target_pairs={{0,2},{2,4},{4,6},{6,8},{8,10},{10,12},{12,14},{14,16},{16,18},{18... | collective-permute-start | bytes 1382408 | tf_op jit(solution)/shard_map/ppermute | solution.py:39
  120.0 0.8 constant_dynamic-update-slice_fusion.4
  120.9 0.8 constant_dynamic-update-slice_fusion.3
  121.7 3.9 collective-permute-done.12
  125.6 7.5 %collective-permute-start.14 = (bf16[40,5760]{1,0:T(8,128)(2,1)S(1)}, bf16[40,5760]{1,0:T(8,128)(2,1)S(1)}, u32[]{:S(2)}, u32[]{:S(2)}) collective-permute-start(bf16[40,5760]{1,0:T(8,128)(2,1)S(1)} %collective-permute-done.12), channel_id=1, source_target_pairs={{0,2},{2,4},{4,6},{6,8},{8,10},{10,12},{12,14},{14,16},{16,18},{18... | collective-permute-start | bytes 1382408 | tf_op jit(solution)/shard_map/ppermute | solution.py:39
  134.0 0.8 constant_dynamic-update-slice_fusion.1
  134.8 3.9 collective-permute-done.14
  139.5 2.5 fusion.11
  142.0 2.5 fusion.13
  144.5 2.5 fusion.15
  147.0 2.5 fusion.17
  149.4 2.5 fusion.19
  151.9 2.5 fusion.21
  154.4 2.5 fusion.25
  156.9 2.5 fusion.23
  159.4 5.9 %fusion.35 = (f32[640]{0:T(1024)S(1)}, f32[640]{0:T(1024)S(1)}, f32[1024,640]{1,0:T(8,128)}) fusion(f32[4,640]{1,0:T(4,128)S(1)} %copy-done.7, f32[4,640]{1,0:T(4,128)S(1)} %copy-done.6, bf16[1,4,16,16,640]{4,3,2,1,0:T(8,128)(2,1)S(1)} %copy-done, f32[640]{0:T(1024)S(1)} %copy-done.12, f32[640]{0:T(1024)S(1)} %copy-done.13, ...), kind=kOutput, calls=%fused_computation.108 | convolution fusion | flops 854588160 | bytes 27064320 | tf_op jit(solution)/shard_map/dot_general | solution.py:69
  165.3 3.2 copy.35
  168.5 4.2 reshape.215
  172.8 5.7 %fusion.36 = (f32[4,32]{0,1:T(8,128)S(1)}, f32[4,32]{0,1:T(8,128)S(1)}) fusion(f32[4,32]{0,1:T(8,128)S(1)} %copy-done.11, f32[4,256,32,20]{1,0,3,2:T(4,128)} %copy.37, f32[4,32]{0,1:T(8,128)S(1)} %copy-done.10, f32[4,256,32,20]{1,0,3,2:T(4,128)} %reshape.215, f32[32,20]{1,0:T(8,128)S(1)} %copy-done.8, f32[32,20]{1,0:T(8,128)S(1)} %copy-done.9), kind=kLoop, calls=%fused_computation.109 | loop fusion | flops 10485504 | bytes 5250048 | tf_op jit(solution)/shard_map/reduce_sum | solution.py:99
  179.0 3.6 multiply_convert_fusion
  182.6 3.2 pad_slice_fusion
  185.8 2.4 bitcast_dynamic-update-slice_fusion.8
  188.2 2.4 bitcast_dynamic-update-slice_fusion.7
  190.7 2.4 bitcast_dynamic-update-slice_fusion.6
  193.1 2.4 bitcast_dynamic-update-slice_fusion.5
  195.5 2.4 bitcast_dynamic-update-slice_fusion.4
  197.9 2.4 bitcast_dynamic-update-slice_fusion.3
  200.3 2.5 bitcast_dynamic-update-slice_fusion.2
  202.8 2.4 bitcast_dynamic-update-slice_fusion.1
  205.2 2.4 bitcast_dynamic-update-slice_fusion
  208.7 1.3 collective-permute-start.15
  210.3 4.9 collective-permute-start.16
  215.2 44.7 %all-reduce.3 = (f32[640]{0:T(1024)S(1)}, f32[640]{0:T(1024)S(1)}) all-reduce(f32[640]{0:T(1024)S(1)} %get-tuple-element.5, f32[640]{0:T(1024)S(1)} %get-tuple-element.4), channel_id=1, replica_groups=mesh['frames'=16,'dp'=2] {'frames','dp'}, use_global_device_ids=true, to_apply=%region_10.11 | all-reduce | flops 1280 | bytes 10240 | tf_op jit(solution)/shard_map/psum | solution.py:97
  261.7 3.0 maximum_select_fusion
  264.7 204.4 %all-reduce.6.cloned.1.call-done = f32[640,5760]{0,1:T(8,128)} async-done(((f32[640,5760]{0,1:T(8,128)}), f32[640,5760]{0,1:T(8,128)}) %all-reduce.6.cloned.1.call-update) | async-done | bytes 14745616
  469.1 5.1 %dynamic-slice_bitcast_fusion = f32[1,20,5760]{1,2,0:T(8,128)} fusion(f32[640,5760]{0,1:T(8,128)} %all-reduce.6.cloned.1.call-done, u32[]{:T(128)S(6)} %multiply.25), kind=kLoop, calls=%fused_computation.16 | loop fusion | bytes 921604
  474.2 2.6 copy.41
  476.8 15.0 %all-gather = f32[2,20,5760]{2,1,0:T(8,128)S(1)} all-gather(f32[1,20,5760]{2,1,0:T(8,128)S(1)} %copy.41), channel_id=1, replica_groups=mesh['frames'=16,'dp'=2] {'dp'}, dimensions={0}, use_global_device_ids=true | all-gather | bytes 1382400 | tf_op jit(solution)/shard_map/all_gather | solution.py:91
  491.9 1.0 reshape.231
  (87 shorter events, 14.4 us)
Async XLA Ops:
  7.2 461.9 %all-reduce.6.cloned.1.call-start = ((), (), s32[]{:S(2)}) async-start(), calls=%async_computation | async-start | bytes 29491200
  7.2 52.5 %collective-permute-start = (bf16[40,5760]{1,0:T(8,128)(2,1)}, bf16[40,5760]{1,0:T(8,128)(2,1)}, u32[]{:S(2)}, u32[]{:S(2)}) collective-permute-start(bf16[40,5760]{1,0:T(8,128)(2,1)} %param.9), channel_id=1, source_target_pairs={{0,2},{2,4},{4,6},{6,8},{8,10},{10,12},{12,14},{14,16},{16,18},{18... | collective-permute-start | bytes 1382408 | tf_op jit(solution)/shard_map/ppermute | solution.py:39
  7.8 52.0 %collective-permute-start.1 = (bf16[40,5760]{1,0:T(8,128)(2,1)}, bf16[40,5760]{1,0:T(8,128)(2,1)S(1)}, u32[]{:S(2)}, u32[]{:S(2)}) collective-permute-start(bf16[40,5760]{1,0:T(8,128)(2,1)} %param.9), channel_id=1, source_target_pairs={{0,30},{2,0},{4,2},{6,4},{8,6},{10,8},{12,10},{14,12},{16,14},{18,... | collective-permute-start | bytes 1382408 | tf_op jit(solution)/shard_map/ppermute | solution.py:44
  14.7 1.9 copy-start.5
  16.7 3.5 copy-start.4
  16.7 4.3 copy-start
  43.7 11.5 %copy-start.12 = (f32[640]{0:T(1024)S(1)}, f32[640]{0:T(1024)}, u32[]{:S(2)}) copy-start(f32[640]{0:T(1024)} %param.11) | copy-start | bytes 7684
  43.7 12.2 %copy-start.13 = (f32[640]{0:T(1024)S(1)}, f32[640]{0:T(1024)}, u32[]{:S(2)}) copy-start(f32[640]{0:T(1024)} %param.10) | copy-start | bytes 7684
  43.7 12.9 %copy-start.2 = (bf16[1,4,16,16,640]{4,3,2,1,0:T(8,128)(2,1)S(1)}, bf16[1,4,16,16,640]{4,3,2,1,0:T(8,128)(2,1)}, u32[]{:S(2)}) copy-start(bf16[1,4,16,16,640]{4,3,2,1,0:T(8,128)(2,1)} %param.8) | copy-start | bytes 3932164
  59.7 11.0 %collective-permute-start.2 = (bf16[40,5760]{1,0:T(8,128)(2,1)}, bf16[40,5760]{1,0:T(8,128)(2,1)S(1)}, u32[]{:S(2)}, u32[]{:S(2)}) collective-permute-start(bf16[40,5760]{1,0:T(8,128)(2,1)} %collective-permute-done), channel_id=1, source_target_pairs={{0,2},{2,4},{4,6},{6,8},{8,10},{10,12},{12,14},{14,16},{16,18},{18... | collective-permute-start | bytes 1382408 | tf_op jit(solution)/shard_map/ppermute | solution.py:39
  59.8 10.9 %collective-permute-start.3 = (bf16[40,5760]{1,0:T(8,128)(2,1)S(1)}, bf16[40,5760]{1,0:T(8,128)(2,1)S(1)}, u32[]{:S(2)}, u32[]{:S(2)}) collective-permute-start(bf16[40,5760]{1,0:T(8,128)(2,1)S(1)} %collective-permute-done.1), channel_id=1, source_target_pairs={{0,30},{2,0},{4,2},{6,4},{8,6},{10,8},{12,10},{14,12},{16,14},{18,... | collective-permute-start | bytes 1382408 | tf_op jit(solution)/shard_map/ppermute | solution.py:44
  70.7 10.7 %collective-permute-start.4 = (bf16[40,5760]{1,0:T(8,128)(2,1)S(1)}, bf16[40,5760]{1,0:T(8,128)(2,1)S(1)}, u32[]{:S(2)}, u32[]{:S(2)}) collective-permute-start(bf16[40,5760]{1,0:T(8,128)(2,1)S(1)} %collective-permute-done.2), channel_id=1, source_target_pairs={{0,2},{2,4},{4,6},{6,8},{8,10},{10,12},{12,14},{14,16},{16,18},{18... | collective-permute-start | bytes 1382408 | tf_op jit(solution)/shard_map/ppermute | solution.py:39
  70.7 11.5 %collective-permute-start.5 = (bf16[40,5760]{1,0:T(8,128)(2,1)S(1)}, bf16[40,5760]{1,0:T(8,128)(2,1)S(1)}, u32[]{:S(2)}, u32[]{:S(2)}) collective-permute-start(bf16[40,5760]{1,0:T(8,128)(2,1)S(1)} %collective-permute-done.3), channel_id=1, source_target_pairs={{0,30},{2,0},{4,2},{6,4},{8,6},{10,8},{12,10},{14,12},{16,14},{18,... | collective-permute-start | bytes 1382408 | tf_op jit(solution)/shard_map/ppermute | solution.py:44
  81.4 10.7 %collective-permute-start.6 = (bf16[40,5760]{1,0:T(8,128)(2,1)S(1)}, bf16[40,5760]{1,0:T(8,128)(2,1)S(1)}, u32[]{:S(2)}, u32[]{:S(2)}) collective-permute-start(bf16[40,5760]{1,0:T(8,128)(2,1)S(1)} %collective-permute-done.4), channel_id=1, source_target_pairs={{0,2},{2,4},{4,6},{6,8},{8,10},{10,12},{12,14},{14,16},{16,18},{18... | collective-permute-start | bytes 1382408 | tf_op jit(solution)/shard_map/ppermute | solution.py:39
  82.2 12.1 %collective-permute-start.7 = (bf16[40,5760]{1,0:T(8,128)(2,1)S(1)}, bf16[40,5760]{1,0:T(8,128)(2,1)S(1)}, u32[]{:S(2)}, u32[]{:S(2)}) collective-permute-start(bf16[40,5760]{1,0:T(8,128)(2,1)S(1)} %collective-permute-done.5), channel_id=1, source_target_pairs={{0,30},{2,0},{4,2},{6,4},{8,6},{10,8},{12,10},{14,12},{16,14},{18,... | collective-permute-start | bytes 1382408 | tf_op jit(solution)/shard_map/ppermute | solution.py:44
  92.1 10.7 %collective-permute-start.8 = (bf16[40,5760]{1,0:T(8,128)(2,1)S(1)}, bf16[40,5760]{1,0:T(8,128)(2,1)S(1)}, u32[]{:S(2)}, u32[]{:S(2)}) collective-permute-start(bf16[40,5760]{1,0:T(8,128)(2,1)S(1)} %collective-permute-done.6), channel_id=1, source_target_pairs={{0,2},{2,4},{4,6},{6,8},{8,10},{10,12},{12,14},{14,16},{16,18},{18... | collective-permute-start | bytes 1382408 | tf_op jit(solution)/shard_map/ppermute | solution.py:39
  94.3 12.9 %collective-permute-start.9 = (bf16[40,5760]{1,0:T(8,128)(2,1)S(1)}, bf16[40,5760]{1,0:T(8,128)(2,1)S(1)}, u32[]{:S(2)}, u32[]{:S(2)}) collective-permute-start(bf16[40,5760]{1,0:T(8,128)(2,1)S(1)} %collective-permute-done.7), channel_id=1, source_target_pairs={{0,30},{2,0},{4,2},{6,4},{8,6},{10,8},{12,10},{14,12},{16,14},{18,... | collective-permute-start | bytes 1382408 | tf_op jit(solution)/shard_map/ppermute | solution.py:44
  102.9 10.7 %collective-permute-start.10 = (bf16[40,5760]{1,0:T(8,128)(2,1)S(1)}, bf16[40,5760]{1,0:T(8,128)(2,1)S(1)}, u32[]{:S(2)}, u32[]{:S(2)}) collective-permute-start(bf16[40,5760]{1,0:T(8,128)(2,1)S(1)} %collective-permute-done.8), channel_id=1, source_target_pairs={{0,2},{2,4},{4,6},{6,8},{8,10},{10,12},{12,14},{14,16},{16,18},{18... | collective-permute-start | bytes 1382408 | tf_op jit(solution)/shard_map/ppermute | solution.py:39
  107.2 12.9 %collective-permute-start.11 = (bf16[40,5760]{1,0:T(8,128)(2,1)S(1)}, bf16[40,5760]{1,0:T(8,128)(2,1)S(1)}, u32[]{:S(2)}, u32[]{:S(2)}) collective-permute-start(bf16[40,5760]{1,0:T(8,128)(2,1)S(1)} %collective-permute-done.9), channel_id=1, source_target_pairs={{0,30},{2,0},{4,2},{6,4},{8,6},{10,8},{12,10},{14,12},{16,14},{18,... | collective-permute-start | bytes 1382408 | tf_op jit(solution)/shard_map/ppermute | solution.py:44
  113.6 12.1 %collective-permute-start.12 = (bf16[40,5760]{1,0:T(8,128)(2,1)S(1)}, bf16[40,5760]{1,0:T(8,128)(2,1)S(1)}, u32[]{:S(2)}, u32[]{:S(2)}) collective-permute-start(bf16[40,5760]{1,0:T(8,128)(2,1)S(1)} %collective-permute-done.10), channel_id=1, source_target_pairs={{0,2},{2,4},{4,6},{6,8},{8,10},{10,12},{12,14},{14,16},{16,18},{18... | collective-permute-start | bytes 1382408 | tf_op jit(solution)/shard_map/ppermute | solution.py:39
  120.0 13.9 %collective-permute-start.13 = (bf16[40,5760]{1,0:T(8,128)(2,1)S(1)}, bf16[40,5760]{1,0:T(8,128)(2,1)S(1)}, u32[]{:S(2)}, u32[]{:S(2)}) collective-permute-start(bf16[40,5760]{1,0:T(8,128)(2,1)S(1)} %collective-permute-done.11), channel_id=1, source_target_pairs={{0,30},{2,0},{4,2},{6,4},{8,6},{10,8},{12,10},{14,12},{16,14},{18,... | collective-permute-start | bytes 1382408 | tf_op jit(solution)/shard_map/ppermute | solution.py:44
  125.6 13.1 %collective-permute-start.14 = (bf16[40,5760]{1,0:T(8,128)(2,1)S(1)}, bf16[40,5760]{1,0:T(8,128)(2,1)S(1)}, u32[]{:S(2)}, u32[]{:S(2)}) collective-permute-start(bf16[40,5760]{1,0:T(8,128)(2,1)S(1)} %collective-permute-done.12), channel_id=1, source_target_pairs={{0,2},{2,4},{4,6},{6,8},{8,10},{10,12},{12,14},{14,16},{16,18},{18... | collective-permute-start | bytes 1382408 | tf_op jit(solution)/shard_map/ppermute | solution.py:39
  156.9 2.5 copy-start.6
  156.9 2.5 copy-start.7
  168.5 4.3 copy-start.8
  168.5 4.3 copy-start.9
  168.5 4.3 copy-start.10
  168.5 4.3 copy-start.11
  182.6 3.2 copy-start.3
  207.6 0.7 copy-start.14
  207.6 0.7 copy-start.15
  208.7 51.9 %collective-permute-start.15 = (bf16[1,80,256]{2,1,0:T(8,128)(2,1)S(1)}, bf16[1,80,256]{2,1,0:T(8,128)(2,1)S(1)}, u32[]{:S(2)}, u32[]{:S(2)}) collective-permute-start(bf16[1,80,256]{2,1,0:T(8,128)(2,1)S(1)} %fusion.5), channel_id=1, source_target_pairs={{2,0},{4,2},{6,4},{8,6},{10,8},{12,10},{14,12},{16,14},{18,16},{20... | collective-permute-start | bytes 122888 | tf_op jit(solution)/shard_map/ppermute | solution.py:18
  210.3 50.7 %collective-permute-start.16 = (bf16[1,80,256]{2,1,0:T(8,128)(2,1)S(1)}, bf16[1,80,256]{2,1,0:T(8,128)(2,1)S(1)}, u32[]{:S(2)}, u32[]{:S(2)}) collective-permute-start(bf16[1,80,256]{2,1,0:T(8,128)(2,1)S(1)} %fusion.6), channel_id=1, source_target_pairs={{0,2},{2,4},{4,6},{6,8},{8,10},{10,12},{12,14},{14,16},{16,18},{18... | collective-permute-start | bytes 122888 | tf_op jit(solution)/shard_map/ppermute | solution.py:17
  259.9 1.8 copy-start.1
Sparse Core Ops, SparseCore 0:
  207.8 261.2 all-reduce.5
